TPU v7x, 256 devices: a whole 4x4x8 slice. The times are simulated.
256 devices in a mesh: dp: 32 (over y, z), tensor: 8 (over x, core).
Axes of the slice: x: 4, y: 4, z: 8, core: 2. Of those that a mesh axis runs over, the one named last changes fastest.
Arguments:
- queries: bfloat16 [256, 6, 8192], P('dp', None, 'tensor'), may hold values from -150 to 150
- new_keys: bfloat16 [256, 6, 1024], P('dp', None, 'tensor'), may hold values from -6 to 6
- new_values: bfloat16 [256, 6, 1024], P('dp', None, 'tensor'), may hold values from -6 to 6
- key_cache: bfloat16 [256, 256, 1024], P('dp', None, 'tensor'), may hold values from -6 to 6
- value_cache: bfloat16 [256, 256, 1024], P('dp', None, 'tensor'), may hold values from -6 to 6
- cache_lengths: int32 [256], P('dp'), may hold values from 32 to 256, as said below
- accepted: int32 [256], P('tensor'), may hold values from 1 to 6
- residual: bfloat16 [256, 6, 8192], P('tensor', None, 'dp'), may hold values from -6 to 6
- out_weight: bfloat16 [8192, 8192], P('tensor', 'dp'), may hold values from -0.0625 to 0.0625
- draft_weight: bfloat16 [8192, 8192], P('tensor', 'dp'), may hold values from -0.0625 to 0.0625
Outputs:
- verified: bfloat16 [256, 6, 8192], P('tensor', None, 'dp')
- drafted: bfloat16 [5, 256, 8192], P(None, 'tensor', 'dp')
Inputs may be any that keep to these rules, and one draw needn't show every extreme that they name: `cache_lengths`: every draw has a window with all 256 slots live.
All inputs are finite; a program needn't handle non-finite values.
Results may differ from a plain program's by a relative error of at most 0.008.
Values may be sent and summed in bfloat16 or wider, within the bound.
No kernel may reach another device: no remote copies, remote signals or barrier semaphores. Data moves between devices by JAX's collectives and lax.ppermute only.
A program may use at most 64 MiB of HBM per device.

v0:
```python
import jax
import jax.numpy as jnp
from jax import lax
from jax.sharding import PartitionSpec as P

HD = 128
STEPS = 5


def spread(block, axis):
    copies = jnp.broadcast_to(block[None], (lax.axis_size(axis),) + block.shape)
    return lax.all_to_all(copies, axis, split_axis=0, concat_axis=0, tiled=True)


def accepted_of_my_windows(accepted):
    dp_size, tensor_size = (lax.axis_size("dp"), lax.axis_size("tensor"))
    ratio = dp_size // tensor_size
    pairs = []
    for j in range(dp_size):
        for i in range(tensor_size):
            source = (ratio * i + j % ratio) * tensor_size + j // ratio
            pairs.append((source, j * tensor_size + i))
    block = lax.ppermute(accepted, ("dp", "tensor"), pairs)
    rows = accepted.shape[0] // ratio
    return lax.dynamic_slice_in_dim(block, lax.axis_index("dp") % ratio * rows, rows, 0)


def pick(rows, accepted):
    chosen = jnp.arange(rows.shape[1])[None, :] == (accepted - 1)[:, None]
    return jnp.sum(
        jnp.where(chosen[:, :, None], rows, jnp.zeros((), rows.dtype)), axis=1, dtype=rows.dtype
    )


def per_device(
    queries,
    new_keys,
    new_values,
    key_cache,
    value_cache,
    cache_lengths,
    accepted,
    residual,
    out_weight,
    draft_weight,
):
    windows_here, tokens_here, query_width = queries.shape
    cache_size = key_cache.shape[1]
    kv_here = new_keys.shape[2] // HD
    group_size = query_width // HD // kv_here
    tensor_size = lax.axis_size("tensor")
    own_accepted = accepted_of_my_windows(accepted)
    draft_columns = lax.all_gather(draft_weight, "tensor", axis=0, tiled=True)
    query_split = queries.reshape(windows_here, tokens_here, kv_here, group_size, HD)
    keys_cached = key_cache.reshape(windows_here, cache_size, kv_here, HD)
    keys_fresh = new_keys.reshape(windows_here, tokens_here, kv_here, HD)
    score_cache = jnp.einsum(
        "wtkgd,wpkd->wkgtp", query_split, keys_cached, preferred_element_type=jnp.float32
    ) * HD ** (-0.5)
    score_fresh = jnp.einsum(
        "wtkgd,wpkd->wkgtp", query_split, keys_fresh, preferred_element_type=jnp.float32
    ) * HD ** (-0.5)
    live_cache = (jnp.arange(cache_size)[None, :] < cache_lengths[:, None])[:, None, None, None, :]
    live_fresh = jnp.arange(tokens_here)[None, :] <= jnp.arange(tokens_here)[:, None]
    scores = jnp.concatenate(
        [
            jnp.where(live_cache, score_cache, -jnp.inf),
            jnp.where(live_fresh, score_fresh, -jnp.inf),
        ],
        axis=-1,
    )
    largest = jnp.max(scores, axis=-1, keepdims=True)
    powered = jnp.exp(scores - largest)
    weights = (powered / jnp.sum(powered, axis=-1, keepdims=True)).astype(jnp.bfloat16)
    values_cached = value_cache.reshape(windows_here, cache_size, kv_here, HD)
    values_fresh = new_values.reshape(windows_here, tokens_here, kv_here, HD)
    mixed_rows = jnp.einsum(
        "wkgtp,wpkd->wtkgd",
        weights[..., :cache_size],
        values_cached,
        preferred_element_type=jnp.float32,
    )
    mixed_rows = mixed_rows + jnp.einsum(
        "wkgtp,wpkd->wtkgd",
        weights[..., cache_size:],
        values_fresh,
        preferred_element_type=jnp.float32,
    )
    attended = mixed_rows.astype(jnp.bfloat16).reshape(windows_here, tokens_here, query_width)
    picked_rows = spread(pick(attended, own_accepted), "dp").reshape(-1, query_width)
    picked_part = jnp.dot(picked_rows, out_weight, preferred_element_type=jnp.float32)
    block_windows, block_tokens, block_cols = residual.shape
    shares = lax.all_to_all(
        picked_part.astype(jnp.bfloat16).reshape(tensor_size, block_windows, block_cols),
        "tensor",
        split_axis=0,
        concat_axis=0,
        tiled=True,
    )
    current = (
        pick(residual, accepted).astype(jnp.float32) + jnp.sum(shares.astype(jnp.float32), axis=0)
    ).astype(jnp.bfloat16)
    partial_out = jnp.dot(
        lax.all_gather(
            attended.reshape(windows_here * tokens_here, query_width), "dp", axis=0, tiled=True
        ),
        out_weight,
        preferred_element_type=jnp.float32,
    )
    summed = lax.psum_scatter(partial_out, "tensor", scatter_dimension=0, tiled=True)
    flat_residual = residual.reshape(block_windows * block_tokens, block_cols).astype(jnp.float32)
    verified = (
        (flat_residual + summed)
        .astype(jnp.bfloat16)
        .reshape(block_windows, block_tokens, block_cols)
    )
    columns = draft_columns.reshape(-1, block_cols, draft_columns.shape[1])
    results = []
    for draft_step in range(STEPS):
        inputs = spread(current, "dp")
        product = jnp.einsum("jwk,jkn->wn", inputs, columns, preferred_element_type=jnp.float32)
        current = jnp.tanh(2.0 * product).astype(jnp.bfloat16)
        results.append(current)
    return (verified, jnp.stack(results))


def solution(mesh):
    placed = (
        P("dp", None, "tensor"),
        P("dp", None, "tensor"),
        P("dp", None, "tensor"),
        P("dp", None, "tensor"),
        P("dp", None, "tensor"),
        P("dp"),
        P("tensor"),
        P("tensor", None, "dp"),
        P("tensor", "dp"),
        P("tensor", "dp"),
    )
    return jax.shard_map(
        per_device,
        mesh=mesh,
        in_specs=placed,
        out_specs=(P("tensor", None, "dp"), P(None, "tensor", "dp")),
        check_vma=False,
    )
```

profile of v0, /device:TPU:32, one launch (start us, length us, event | category | flops | bytes accessed | tf_op | source)
XLA Modules:
  0.0 202.9 jit_solution(7244637274583813440)
XLA Ops:
  7.2 0.0 copy-start
  7.2 0.0 copy-start.5
  7.2 0.0 copy-start.3
  7.2 0.0 all-gather.5.cloned.1.call-start
  7.2 0.7 all-gather.5.cloned.1.call-update
  7.9 0.0 all-gather.3.cloned.1.call-start
  8.0 1.3 collective-permute-start
  9.3 0.7 iota_compare_fusion
  10.0 1.2 fusion.35
  11.2 1.4 fusion.34
  12.6 0.3 fusion.27
  12.9 0.2 divide_convert_fusion
  13.1 0.9 fusion.28
  14.0 0.0 collective-permute-done
  14.0 0.1 dynamic-slice_add_fusion
  14.0 0.1 iota_compare_fusion.1
  14.1 1.3 fusion.29
  15.4 0.7 copy.53
  16.0 0.0 all-gather.3.cloned.1.call-update
  16.1 0.9 broadcast_in_dim.104
  16.9 19.1 %all-to-all-start = ((bf16[32,8,1024]{2,1,0:T(8,128)(2,1)}), bf16[32,8,1024]{2,1,0:T(8,128)(2,1)S(1)}, u32[]{:S(2)}, u32[]{:S(2)}) async-start(bf16[32,8,1024]{2,1,0:T(8,128)(2,1)} %broadcast_in_dim.104), calls=%async_computation.1 | async-start | bytes 1048576 | tf_op jit(solution)/shard_map/all_to_all | solution.py:12
  36.0 0.0 copy-done.5
  36.1 15.0 %all-to-all-done = bf16[32,8,1024]{2,1,0:T(8,128)(2,1)S(1)} async-done(((bf16[32,8,1024]{2,1,0:T(8,128)(2,1)}), bf16[32,8,1024]{2,1,0:T(8,128)(2,1)S(1)}, u32[]{:S(2)}, u32[]{:S(2)}) %all-to-all-start) | async-done | bytes 524320 | tf_op jit(solution)/shard_map/all_to_all | solution.py:12
  51.1 0.0 copy-done
  51.1 1.0 convolution_convert_fusion
  52.0 3.4 %all-to-all-start.1 = ((bf16[8,32,256]{2,1,0:T(8,128)(2,1)}), bf16[8,32,256]{2,1,0:T(8,128)(2,1)S(1)}, u32[]{:S(2)}, u32[]{:S(2)}) async-start(bf16[8,32,256]{2,1,0:T(8,128)(2,1)} %bitcast.19), calls=%async_computation.2 | async-start | bytes 262144 | tf_op jit(solution)/shard_map/all_to_all | solution.py:93
  55.4 0.0 copy-done.3
  55.4 0.1 select_reduce_fusion
  55.5 5.9 %all-to-all-done.1 = bf16[8,32,256]{2,1,0:T(8,128)(2,1)S(1)} async-done(((bf16[8,32,256]{2,1,0:T(8,128)(2,1)}), bf16[8,32,256]{2,1,0:T(8,128)(2,1)S(1)}, u32[]{:S(2)}, u32[]{:S(2)}) %all-to-all-start.1) | async-done | bytes 131104 | tf_op jit(solution)/shard_map/all_to_all | solution.py:93
  61.5 0.1 broadcast_in_dim.105
  61.6 23.8 %all_to_all.35 = bf16[32,32,256]{2,1,0:T(8,128)(2,1)S(1)} all-to-all(bf16[32,32,256]{2,1,0:T(8,128)(2,1)S(1)} %broadcast_in_dim.105), channel_id=1, replica_groups=mesh['dp'=32,'tensor'=8] {'dp'}, dimensions={0} | all-to-all | bytes 1048576 | tf_op jit(solution)/shard_map/all_to_all | solution.py:12
  85.4 0.0 all-gather.5.cloned.1.call-done
  85.4 0.0 copy-start.1
  85.4 3.2 %bitcast_dynamic-update-slice_fusion.3 = (bf16[5,32,256]{2,1,0:T(8,128)(2,1)S(1)}, bf16[32,256]{1,0:T(8,128)(2,1)S(1)}) fusion(bf16[32,32,256]{2,1,0:T(8,128)(2,1)S(1)} %all_to_all.35, bf16[32,256,256]{2,1,0:T(8,128)(2,1)} %bitcast.131), kind=kOutput, calls=%fused_computation.55 | convolution fusion | flops 134234112 | bytes 4751360 | tf_op jit(solution)/shard_map/jwk,jkn->wn/dot_general | solution.py:121
  88.5 0.1 broadcast_in_dim.106
  88.6 23.2 %all_to_all.36 = bf16[32,32,256]{2,1,0:T(8,128)(2,1)S(1)} all-to-all(bf16[32,32,256]{2,1,0:T(8,128)(2,1)S(1)} %broadcast_in_dim.106), channel_id=1, replica_groups=mesh['dp'=32,'tensor'=8] {'dp'}, dimensions={0} | all-to-all | bytes 1048576 | tf_op jit(solution)/shard_map/all_to_all | solution.py:12
  111.8 0.0 copy-done.1
  111.9 0.8 bitcast_dynamic-update-slice_fusion.2
  112.7 0.9 broadcast_in_dim.107
  113.6 5.5 %all-to-all-start.4 = ((bf16[32,32,256]{2,1,0:T(8,128)(2,1)}), bf16[32,32,256]{2,1,0:T(8,128)(2,1)S(1)}, u32[]{:S(2)}, u32[]{:S(2)}) async-start(bf16[32,32,256]{2,1,0:T(8,128)(2,1)} %broadcast_in_dim.107), calls=%async_computation.5 | async-start | bytes 1048576 | tf_op jit(solution)/shard_map/all_to_all | solution.py:12
  119.1 0.0 reduce-scatter.2.cloned.1.call-start
  119.2 18.9 %all-gather.3.cloned.1.call-done = bf16[1536,1024]{1,0:T(8,128)(2,1)} async-done(((bf16[48,1024]{1,0:T(8,128)(2,1)}), bf16[1536,1024]{1,0:T(8,128)(2,1)}) %all-gather.3.cloned.1.call-update) | async-done | bytes 3145744 | tf_op jit(solution)/shard_map/all_gather | solution.py:104
  138.1 4.1 %fusion.36 = f32[1536,256]{1,0:T(8,128)} fusion(bf16[1536,1024]{1,0:T(8,128)(2,1)} %all-gather.3.cloned.1.call-done, bf16[1024,256]{1,0:T(8,128)(2,1)S(1)} %copy-done), kind=kOutput, calls=%fused_computation.66 | convolution fusion | flops 805306368 | bytes 5242880 | tf_op jit(solution)/shard_map/dot_general | solution.py:103
  142.2 0.0 reduce-scatter.2.cloned.1.call-update
  142.2 0.0 all-to-all-done.4
  142.2 0.0 copy-start.2
  142.2 3.2 %bitcast_dynamic-update-slice_fusion.1 = (bf16[5,32,256]{2,1,0:T(8,128)(2,1)S(1)}, bf16[32,256]{1,0:T(8,128)(2,1)S(1)}) fusion(bf16[5,32,256]{2,1,0:T(8,128)(2,1)S(1)} %get-tuple-element.14, bf16[32,32,256]{2,1,0:T(8,128)(2,1)S(1)} %all-to-all-done.4, bf16[32,256,256]{2,1,0:T(8,128)(2,1)} %bitcast.132), kind=kOutput, calls=%fused_computation.53 | convolution fusion | flops 134234112 | bytes 4751360 | tf_op jit(solution)/shard_map/jwk,jkn->wn/dot_general | solution.py:121
  145.4 0.1 broadcast_in_dim.108
  145.5 24.1 %all_to_all.37 = bf16[32,32,256]{2,1,0:T(8,128)(2,1)S(1)} all-to-all(bf16[32,32,256]{2,1,0:T(8,128)(2,1)S(1)} %broadcast_in_dim.108), channel_id=1, replica_groups=mesh['dp'=32,'tensor'=8] {'dp'}, dimensions={0} | all-to-all | bytes 1048576 | tf_op jit(solution)/shard_map/all_to_all | solution.py:12
  169.6 0.0 copy-done.2
  169.6 0.8 bitcast_dynamic-update-slice_fusion
  170.4 0.9 broadcast_in_dim.109
  171.3 4.8 %all-to-all-start.6 = ((bf16[32,32,256]{2,1,0:T(8,128)(2,1)}), bf16[32,32,256]{2,1,0:T(8,128)(2,1)S(1)}, u32[]{:S(2)}, u32[]{:S(2)}) async-start(bf16[32,32,256]{2,1,0:T(8,128)(2,1)} %broadcast_in_dim.109), calls=%async_computation.7 | async-start | bytes 1048576 | tf_op jit(solution)/shard_map/all_to_all | solution.py:12
  176.2 0.1 copy.19
  176.3 0.2 reduce-scatter.2.cloned.1.call-done
  176.5 0.9 add_convert_fusion
  177.5 0.7 copy.25
  178.1 14.5 %all-to-all-done.6 = bf16[32,32,256]{2,1,0:T(8,128)(2,1)S(1)} async-done(((bf16[32,32,256]{2,1,0:T(8,128)(2,1)}), bf16[32,32,256]{2,1,0:T(8,128)(2,1)S(1)}, u32[]{:S(2)}, u32[]{:S(2)}) %all-to-all-start.6) | async-done | bytes 524320 | tf_op jit(solution)/shard_map/all_to_all | solution.py:12
  192.7 3.0 %fusion.22 = bf16[5,32,256]{2,1,0:T(8,128)(2,1)S(1)} fusion(bf16[5,32,256]{2,1,0:T(8,128)(2,1)S(1)} %get-tuple-element.18, bf16[32,32,256]{2,1,0:T(8,128)(2,1)S(1)} %all-to-all-done.6, bf16[32,256,256]{2,1,0:T(8,128)(2,1)} %bitcast.133), kind=kOutput, calls=%fused_computation.31 | convolution fusion | flops 134234112 | bytes 4734976 | tf_op jit(solution)/shard_map/jwk,jkn->wn/dot_general | solution.py:121
  195.7 0.0 copy-start.4
  195.7 0.6 copy-done.4
  (9 shorter events, 0.1 us)
Async XLA Ops:
  7.2 43.9 %copy-start = (bf16[1024,256]{1,0:T(8,128)(2,1)S(1)}, bf16[1024,256]{1,0:T(8,128)(2,1)}, u32[]{:S(2)}) copy-start(bf16[1024,256]{1,0:T(8,128)(2,1)} %param.18) | copy-start | bytes 1572868
  7.2 28.9 %copy-start.5 = (s32[32]{0:T(128)S(1)}, s32[32]{0:T(128)}, u32[]{:S(2)}) copy-start(s32[32]{0:T(128)} %param.16) | copy-start | bytes 388
  7.2 48.2 %copy-start.3 = (bf16[32,6,256]{2,0,1:T(8,128)(2,1)S(1)}, bf16[32,6,256]{2,0,1:T(8,128)(2,1)}, u32[]{:S(2)}) copy-start(bf16[32,6,256]{2,0,1:T(8,128)(2,1)} %param.17) | copy-start | bytes 294916
  7.2 78.2 %all-gather.5.cloned.1.call-start = ((), (), s32[]{:S(2)}) async-start(), calls=%async_computation.10 | async-start | bytes 4718592 | tf_op jit(solution)/shard_map/all_gather | solution.py:53
  7.9 130.1 %all-gather.3.cloned.1.call-start = ((), (), s32[]{:S(2)}) async-start(), calls=%async_computation.8 | async-start | bytes 3244032 | tf_op jit(solution)/shard_map/all_gather | solution.py:104
  8.0 6.0 %collective-permute-start = (s32[32]{0:T(128)}, s32[32]{0:T(128)S(1)}, u32[]{:S(2)}, u32[]{:S(2)}) collective-permute-start(s32[32]{0:T(128)} %param.16), channel_id=1, source_target_pairs={{0,0},{32,1},{64,2},{96,3},{128,4},{160,5},{192,6},{224,7},{8,8},{... | collective-permute-start | bytes 392 | tf_op jit(solution)/shard_map/ppermute | solution.py:23
  16.9 34.2 %all-to-all-start = ((bf16[32,8,1024]{2,1,0:T(8,128)(2,1)}), bf16[32,8,1024]{2,1,0:T(8,128)(2,1)S(1)}, u32[]{:S(2)}, u32[]{:S(2)}) async-start(bf16[32,8,1024]{2,1,0:T(8,128)(2,1)} %broadcast_in_dim.104), calls=%async_computation.1 | async-start | bytes 1048576 | tf_op jit(solution)/shard_map/all_to_all | solution.py:12
  52.0 9.4 %all-to-all-start.1 = ((bf16[8,32,256]{2,1,0:T(8,128)(2,1)}), bf16[8,32,256]{2,1,0:T(8,128)(2,1)S(1)}, u32[]{:S(2)}, u32[]{:S(2)}) async-start(bf16[8,32,256]{2,1,0:T(8,128)(2,1)} %bitcast.19), calls=%async_computation.2 | async-start | bytes 262144 | tf_op jit(solution)/shard_map/all_to_all | solution.py:93
  85.4 26.5 %copy-start.1 = (bf16[8192,256]{1,0:T(8,128)(2,1)S(1)}, bf16[8192,256]{1,0:T(8,128)(2,1)}, u32[]{:S(2)}) copy-start(bf16[8192,256]{1,0:T(8,128)(2,1)} %all-gather.5.cloned.1.call-done) | copy-start | bytes 12582916
  113.6 28.6 %all-to-all-start.4 = ((bf16[32,32,256]{2,1,0:T(8,128)(2,1)}), bf16[32,32,256]{2,1,0:T(8,128)(2,1)S(1)}, u32[]{:S(2)}, u32[]{:S(2)}) async-start(bf16[32,32,256]{2,1,0:T(8,128)(2,1)} %broadcast_in_dim.107), calls=%async_computation.5 | async-start | bytes 1048576 | tf_op jit(solution)/shard_map/all_to_all | solution.py:12
  119.1 57.4 %reduce-scatter.2.cloned.1.call-start = ((), (), s32[]{:S(2)}) async-start(), calls=%async_computation.9 | async-start | bytes 1769472 | tf_op jit(solution)/shard_map/reduce_scatter | solution.py:110
  142.2 27.4 %copy-start.2 = (bf16[8192,256]{1,0:T(8,128)(2,1)S(1)}, bf16[8192,256]{1,0:T(8,128)(2,1)}, u32[]{:S(2)}) copy-start(bf16[8192,256]{1,0:T(8,128)(2,1)} %all-gather.5.cloned.1.call-done) | copy-start | bytes 12582916
  171.3 21.4 %all-to-all-start.6 = ((bf16[32,32,256]{2,1,0:T(8,128)(2,1)}), bf16[32,32,256]{2,1,0:T(8,128)(2,1)S(1)}, u32[]{:S(2)}, u32[]{:S(2)}) async-start(bf16[32,32,256]{2,1,0:T(8,128)(2,1)} %broadcast_in_dim.109), calls=%async_computation.7 | async-start | bytes 1048576 | tf_op jit(solution)/shard_map/all_to_all | solution.py:12
  195.7 0.6 copy-start.4
Sparse Core Ops, SparseCore 0:
  9.9 37.2 all-gather.4
  50.4 87.6 all-gather.2
  142.3 34.1 reduce-scatter.1
where the time goes:
time: 204 us; the launch traced here: 203 us
  blocking collectives  71.2 us (35%)
  waiting for transfers between devices  55.3 us (27%)
  starting transfers between devices  34.3 us (17%)
  matrix products  20.8 us (10%)
  between operations  14 us (7%)
  local copies, waits for them, and re-layouts  4.89 us (2%)
  other arithmetic  2.43 us (1%)
    all_to_all x3, blocking collectives, spread(): return lax.all_to_all(copies, axis, split_axis=0, concat_axis=0, tiled=True)  71.2 us
    all_to_all x3, waiting for transfers between devices, spread(): return lax.all_to_all(copies, axis, split_axis=0, concat_axis=0, tiled=True)  29.5 us
    all_to_all x3, starting transfers between devices, spread(): return lax.all_to_all(copies, axis, split_axis=0, concat_axis=0, tiled=True)  29.5 us
    all_gather x1, waiting for transfers between devices, per_device(): lax.all_gather(attended.reshape(windows_here * tokens_here, query_width),...  18.9 us
    dot_general x5, matrix products, per_device(): jnp.einsum('jwk,jkn->wn', inputs, columns, preferred_element_type=jnp.flo...  11 us
    all_to_all x1, waiting for transfers between devices, per_device(): lax.all_to_all(picked_part.astype(jnp.bfloat16).reshape(tensor_size, bloc...  5.94 us
    dot_general x1, matrix products, per_device(): jnp.dot(lax.all_gather(attended.reshape(windows_here * tokens_here, query...  4.12 us
  transfers between devices with their start and end apart: 8, of which 5 were waited for; matrix products, arithmetic and copies ran while one was open for 12% of the time, Pallas kernels for 0%

commit v1 on v0

--- a/solution.py
+++ b/solution.py
@@ -101,8 +101,17 @@
         pick(residual, accepted).astype(jnp.float32) + jnp.sum(shares.astype(jnp.float32), axis=0)
     ).astype(jnp.bfloat16)
     partial_out = jnp.dot(
-        lax.all_gather(
-            attended.reshape(windows_here * tokens_here, query_width), "dp", axis=0, tiled=True
+        jnp.concatenate(
+            lax.all_to_all(
+                jnp.stack(
+                    [attended.reshape(windows_here * tokens_here, query_width)]
+                    * lax.axis_size("dp")
+                ),
+                "dp",
+                0,
+                0,
+            ),
+            0,
         ),
         out_weight,
         preferred_element_type=jnp.float32,

time: 204 us -> 272 us (1.33)
  waiting for transfers between devices: 55.3 us -> 134 us
  blocking collectives: 71.2 us -> 43.6 us
  starting transfers between devices: 34.3 us -> 46.5 us
    all_to_all x0 -> x1, waiting for transfers between devices: none -> 67.1 us  [per_device(): lax.all_to_all(jnp.stack([attended.reshape(windows_here * tokens_here, qu...]
    all_to_all x3 -> x4, waiting for transfers between devices: 29.5 us -> 60.1 us  [spread(): return lax.all_to_all(copies, axis, split_axis=0, concat_axis=0, tiled=True)]
    all_to_all x3 -> x2, blocking collectives: 71.2 us -> 43.6 us  [spread(): return lax.all_to_all(copies, axis, split_axis=0, concat_axis=0, tiled=True)]
    all_gather x1 -> x0, waiting for transfers between devices: 18.9 us -> none  [per_device(): lax.all_gather(attended.reshape(windows_here * tokens_here, query_width),...]
    all_to_all x3 -> x4, starting transfers between devices: 29.5 us -> 36.8 us  [spread(): return lax.all_to_all(copies, axis, split_axis=0, concat_axis=0, tiled=True)]
    all_to_all x0 -> x1, starting transfers between devices: none -> 4.91 us  [per_device(): lax.all_to_all(jnp.stack([attended.reshape(windows_here * tokens_here, qu...]
  transfers between devices with their start and end apart: 8 -> 9, of which waited for: 5 -> 6; matrix products, arithmetic and copies ran while one was open for 12% -> 8% of each run, Pallas kernels for 0% -> 0%
where the time goes in v1:
time: 272 us; the launch traced here: 271 us
  waiting for transfers between devices  134 us (49%)
  starting transfers between devices  46.5 us (17%)
  blocking collectives  43.6 us (16%)
  matrix products  22.8 us (8%)
  between operations  14.3 us (5%)
  local copies, waits for them, and re-layouts  7.17 us (3%)
    all_to_all x1, waiting for transfers between devices, per_device(): lax.all_to_all(jnp.stack([attended.reshape(windows_here * tokens_here, qu...  67.1 us
    all_to_all x4, waiting for transfers between devices, spread(): return lax.all_to_all(copies, axis, split_axis=0, concat_axis=0, tiled=True)  60.1 us
    all_to_all x2, blocking collectives, spread(): return lax.all_to_all(copies, axis, split_axis=0, concat_axis=0, tiled=True)  43.6 us
    all_to_all x4, starting transfers between devices, spread(): return lax.all_to_all(copies, axis, split_axis=0, concat_axis=0, tiled=True)  36.8 us
    dot_general x5, matrix products, per_device(): jnp.einsum('jwk,jkn->wn', inputs, columns, preferred_element_type=jnp.flo...  13.1 us
    all_to_all x1, waiting for transfers between devices, per_device(): lax.all_to_all(picked_part.astype(jnp.bfloat16).reshape(tensor_size, bloc...  5.94 us
  transfers between devices with their start and end apart: 9, of which 6 were waited for; matrix products, arithmetic and copies ran while one was open for 8% of the time, Pallas kernels for 0%

profile of v1, /device:TPU:32, one launch (start us, length us, event | category | flops | bytes accessed | tf_op | source)
XLA Modules:
  0.0 270.8 jit_solution(97152685743779370)
XLA Ops:
  7.2 0.0 copy-start
  7.2 0.0 copy-start.4
  7.2 0.0 copy-start.2
  7.2 0.0 all-gather.2.cloned.1.call-start
  7.2 0.7 all-gather.2.cloned.1.call-update
  7.9 1.3 collective-permute-start
  9.3 0.7 iota_compare_fusion
  10.0 1.2 fusion.35
  11.1 1.4 fusion.34
  12.6 0.3 fusion.27
  12.9 0.2 divide_convert_fusion
  13.0 0.9 fusion.28
  13.9 0.0 collective-permute-done
  13.9 0.1 dynamic-slice_add_fusion
  14.0 0.1 iota_compare_fusion.1
  14.1 1.3 fusion.29
  15.3 0.9 broadcast_in_dim.104
  16.2 19.1 %all-to-all-start.1 = ((bf16[32,8,1024]{2,1,0:T(8,128)(2,1)}), bf16[32,8,1024]{2,1,0:T(8,128)(2,1)S(1)}, u32[]{:S(2)}, u32[]{:S(2)}) async-start(bf16[32,8,1024]{2,1,0:T(8,128)(2,1)} %broadcast_in_dim.104), calls=%async_computation.2 | async-start | bytes 1048576 | tf_op jit(solution)/shard_map/all_to_all | solution.py:12
  35.3 0.0 copy-done.4
  35.4 15.0 %all-to-all-done.1 = bf16[32,8,1024]{2,1,0:T(8,128)(2,1)S(1)} async-done(((bf16[32,8,1024]{2,1,0:T(8,128)(2,1)}), bf16[32,8,1024]{2,1,0:T(8,128)(2,1)S(1)}, u32[]{:S(2)}, u32[]{:S(2)}) %all-to-all-start.1) | async-done | bytes 524320 | tf_op jit(solution)/shard_map/all_to_all | solution.py:12
  50.4 0.0 copy-done
  50.4 0.9 convolution_convert_fusion
  51.3 3.4 %all-to-all-start.2 = ((bf16[8,32,256]{2,1,0:T(8,128)(2,1)}), bf16[8,32,256]{2,1,0:T(8,128)(2,1)S(1)}, u32[]{:S(2)}, u32[]{:S(2)}) async-start(bf16[8,32,256]{2,1,0:T(8,128)(2,1)} %bitcast.20), calls=%async_computation.3 | async-start | bytes 262144 | tf_op jit(solution)/shard_map/all_to_all | solution.py:93
  54.7 0.0 copy-done.2
  54.7 0.1 select_reduce_fusion
  54.8 5.9 %all-to-all-done.2 = bf16[8,32,256]{2,1,0:T(8,128)(2,1)S(1)} async-done(((bf16[8,32,256]{2,1,0:T(8,128)(2,1)}), bf16[8,32,256]{2,1,0:T(8,128)(2,1)S(1)}, u32[]{:S(2)}, u32[]{:S(2)}) %all-to-all-start.2) | async-done | bytes 131104 | tf_op jit(solution)/shard_map/all_to_all | solution.py:93
  60.8 0.1 broadcast_in_dim.105
  60.8 22.1 %all_to_all.40 = bf16[32,32,256]{2,1,0:T(8,128)(2,1)S(1)} all-to-all(bf16[32,32,256]{2,1,0:T(8,128)(2,1)S(1)} %broadcast_in_dim.105), channel_id=1, replica_groups=mesh['dp'=32,'tensor'=8] {'dp'}, dimensions={0} | all-to-all | bytes 1048576 | tf_op jit(solution)/shard_map/all_to_all | solution.py:12
  82.9 0.0 all-gather.2.cloned.1.call-done
  82.9 3.0 %bitcast_dynamic-update-slice_fusion.3 = (bf16[5,32,256]{2,1,0:T(8,128)(2,1)S(1)}, bf16[32,256]{1,0:T(8,128)(2,1)S(1)}) fusion(bf16[32,32,256]{2,1,0:T(8,128)(2,1)S(1)} %all_to_all.40, bf16[32,256,256]{2,1,0:T(8,128)(2,1)} %bitcast.132), kind=kOutput, calls=%fused_computation.55 | convolution fusion | flops 134234112 | bytes 4751360 | tf_op jit(solution)/shard_map/jwk,jkn->wn/dot_general | solution.py:130
  86.0 0.9 broadcast_in_dim.106
  86.8 4.8 %all-to-all-start.4 = ((bf16[32,32,256]{2,1,0:T(8,128)(2,1)}), bf16[32,32,256]{2,1,0:T(8,128)(2,1)S(1)}, u32[]{:S(2)}, u32[]{:S(2)}) async-start(bf16[32,32,256]{2,1,0:T(8,128)(2,1)} %broadcast_in_dim.106), calls=%async_computation.5 | async-start | bytes 1048576 | tf_op jit(solution)/shard_map/all_to_all | solution.py:12
  91.7 16.9 %all-to-all-done.4 = bf16[32,32,256]{2,1,0:T(8,128)(2,1)S(1)} async-done(((bf16[32,32,256]{2,1,0:T(8,128)(2,1)}), bf16[32,32,256]{2,1,0:T(8,128)(2,1)S(1)}, u32[]{:S(2)}, u32[]{:S(2)}) %all-to-all-start.4) | async-done | bytes 524320 | tf_op jit(solution)/shard_map/all_to_all | solution.py:12
  108.6 2.1 stack.21
  110.7 4.9 %all-to-all-start = ((bf16[32,48,1024]{2,1,0:T(8,128)(2,1)}), bf16[32,48,1024]{2,1,0:T(8,128)(2,1)}, u32[]{:S(2)}, u32[]{:S(2)}) async-start(bf16[32,48,1024]{2,1,0:T(8,128)(2,1)} %stack.21), calls=%async_computation | async-start | bytes 6291456 | tf_op jit(solution)/shard_map/all_to_all | solution.py:105
  115.6 3.0 %bitcast_dynamic-update-slice_fusion.2 = (bf16[5,32,256]{2,1,0:T(8,128)(2,1)S(1)}, bf16[32,256]{1,0:T(8,128)(2,1)S(1)}) fusion(bf16[5,32,256]{2,1,0:T(8,128)(2,1)S(1)} %get-tuple-element.12, bf16[32,32,256]{2,1,0:T(8,128)(2,1)S(1)} %all-to-all-done.4, bf16[32,256,256]{2,1,0:T(8,128)(2,1)} %bitcast.133), kind=kOutput, calls=%fused_computation.54 | convolution fusion | flops 134234112 | bytes 4751360 | tf_op jit(solution)/shard_map/jwk,jkn->wn/dot_general | solution.py:130
  118.6 67.1 %all-to-all-done = bf16[32,48,1024]{2,1,0:T(8,128)(2,1)} async-done(((bf16[32,48,1024]{2,1,0:T(8,128)(2,1)}), bf16[32,48,1024]{2,1,0:T(8,128)(2,1)}, u32[]{:S(2)}, u32[]{:S(2)}) %all-to-all-start) | async-done | bytes 3145760 | tf_op jit(solution)/shard_map/all_to_all | solution.py:105
  185.8 0.9 broadcast_in_dim.107
  186.7 8.0 %all-to-all-start.5 = ((bf16[32,32,256]{2,1,0:T(8,128)(2,1)}), bf16[32,32,256]{2,1,0:T(8,128)(2,1)S(1)}, u32[]{:S(2)}, u32[]{:S(2)}) async-start(bf16[32,32,256]{2,1,0:T(8,128)(2,1)} %broadcast_in_dim.107), calls=%async_computation.6 | async-start | bytes 1048576 | tf_op jit(solution)/shard_map/all_to_all | solution.py:12
  194.7 0.0 reduce-scatter.2.cloned.1.call-start
  194.8 4.1 %fusion.36 = f32[1536,256]{1,0:T(8,128)} fusion(bf16[1536,1024]{1,0:T(8,128)(2,1)} %bitcast.16, bf16[1024,256]{1,0:T(8,128)(2,1)S(1)} %copy-done), kind=kOutput, calls=%fused_computation.66 | convolution fusion | flops 805306368 | bytes 5242880 | tf_op jit(solution)/shard_map/dot_general | solution.py:103
  198.9 0.0 reduce-scatter.2.cloned.1.call-update
  198.9 13.3 %all-to-all-done.5 = bf16[32,32,256]{2,1,0:T(8,128)(2,1)S(1)} async-done(((bf16[32,32,256]{2,1,0:T(8,128)(2,1)}), bf16[32,32,256]{2,1,0:T(8,128)(2,1)S(1)}, u32[]{:S(2)}, u32[]{:S(2)}) %all-to-all-start.5) | async-done | bytes 524320 | tf_op jit(solution)/shard_map/all_to_all | solution.py:12
  212.2 0.0 copy-start.1
  212.2 3.2 %bitcast_dynamic-update-slice_fusion.1 = (bf16[5,32,256]{2,1,0:T(8,128)(2,1)S(1)}, bf16[32,256]{1,0:T(8,128)(2,1)S(1)}) fusion(bf16[5,32,256]{2,1,0:T(8,128)(2,1)S(1)} %get-tuple-element.14, bf16[32,32,256]{2,1,0:T(8,128)(2,1)S(1)} %all-to-all-done.5, bf16[32,256,256]{2,1,0:T(8,128)(2,1)} %bitcast.134), kind=kOutput, calls=%fused_computation.53 | convolution fusion | flops 134234112 | bytes 4751360 | tf_op jit(solution)/shard_map/jwk,jkn->wn/dot_general | solution.py:130
  215.4 0.1 broadcast_in_dim.108
  215.5 21.5 %all_to_all.41 = bf16[32,32,256]{2,1,0:T(8,128)(2,1)S(1)} all-to-all(bf16[32,32,256]{2,1,0:T(8,128)(2,1)S(1)} %broadcast_in_dim.108), channel_id=1, replica_groups=mesh['dp'=32,'tensor'=8] {'dp'}, dimensions={0} | all-to-all | bytes 1048576 | tf_op jit(solution)/shard_map/all_to_all | solution.py:12
  237.0 0.0 copy-done.1
  237.0 0.8 bitcast_dynamic-update-slice_fusion
  237.8 0.9 broadcast_in_dim.109
  238.7 4.9 %all-to-all-start.7 = ((bf16[32,32,256]{2,1,0:T(8,128)(2,1)}), bf16[32,32,256]{2,1,0:T(8,128)(2,1)S(1)}, u32[]{:S(2)}, u32[]{:S(2)}) async-start(bf16[32,32,256]{2,1,0:T(8,128)(2,1)} %broadcast_in_dim.109), calls=%async_computation.8 | async-start | bytes 1048576 | tf_op jit(solution)/shard_map/all_to_all | solution.py:12
  243.6 0.1 copy.19
  243.7 0.0 reduce-scatter.2.cloned.1.call-done
  243.7 0.9 add_convert_fusion
  244.7 0.7 copy.25
  245.4 14.9 %all-to-all-done.7 = bf16[32,32,256]{2,1,0:T(8,128)(2,1)S(1)} async-done(((bf16[32,32,256]{2,1,0:T(8,128)(2,1)}), bf16[32,32,256]{2,1,0:T(8,128)(2,1)S(1)}, u32[]{:S(2)}, u32[]{:S(2)}) %all-to-all-start.7) | async-done | bytes 524320 | tf_op jit(solution)/shard_map/all_to_all | solution.py:12
  260.3 3.0 %fusion.22 = bf16[5,32,256]{2,1,0:T(8,128)(2,1)S(1)} fusion(bf16[5,32,256]{2,1,0:T(8,128)(2,1)S(1)} %get-tuple-element.18, bf16[32,32,256]{2,1,0:T(8,128)(2,1)S(1)} %all-to-all-done.7, bf16[32,256,256]{2,1,0:T(8,128)(2,1)} %bitcast.135), kind=kOutput, calls=%fused_computation.31 | convolution fusion | flops 134234112 | bytes 4734976 | tf_op jit(solution)/shard_map/jwk,jkn->wn/dot_general | solution.py:130
  263.3 0.0 copy-start.3
  263.4 0.6 copy-done.3
  (10 shorter events, 0.1 us)
Async XLA Ops:
  7.2 43.2 %copy-start = (bf16[1024,256]{1,0:T(8,128)(2,1)S(1)}, bf16[1024,256]{1,0:T(8,128)(2,1)}, u32[]{:S(2)}) copy-start(bf16[1024,256]{1,0:T(8,128)(2,1)} %param.18) | copy-start | bytes 1572868
  7.2 28.1 %copy-start.4 = (s32[32]{0:T(128)S(1)}, s32[32]{0:T(128)}, u32[]{:S(2)}) copy-start(s32[32]{0:T(128)} %param.16) | copy-start | bytes 388
  7.2 47.5 %copy-start.2 = (bf16[32,6,256]{2,0,1:T(8,128)(2,1)S(1)}, bf16[32,6,256]{2,0,1:T(8,128)(2,1)}, u32[]{:S(2)}) copy-start(bf16[32,6,256]{2,0,1:T(8,128)(2,1)} %param.17) | copy-start | bytes 294916
  7.2 75.7 %all-gather.2.cloned.1.call-start = ((), (), s32[]{:S(2)}) async-start(), calls=%async_computation.10 | async-start | bytes 4718592 | tf_op jit(solution)/shard_map/all_gather | solution.py:53
  7.9 6.0 %collective-permute-start = (s32[32]{0:T(128)}, s32[32]{0:T(128)S(1)}, u32[]{:S(2)}, u32[]{:S(2)}) collective-permute-start(s32[32]{0:T(128)} %param.16), channel_id=1, source_target_pairs={{0,0},{32,1},{64,2},{96,3},{128,4},{160,5},{192,6},{224,7},{8,8},{... | collective-permute-start | bytes 392 | tf_op jit(solution)/shard_map/ppermute | solution.py:23
  16.2 34.2 %all-to-all-start.1 = ((bf16[32,8,1024]{2,1,0:T(8,128)(2,1)}), bf16[32,8,1024]{2,1,0:T(8,128)(2,1)S(1)}, u32[]{:S(2)}, u32[]{:S(2)}) async-start(bf16[32,8,1024]{2,1,0:T(8,128)(2,1)} %broadcast_in_dim.104), calls=%async_computation.2 | async-start | bytes 1048576 | tf_op jit(solution)/shard_map/all_to_all | solution.py:12
  51.3 9.4 %all-to-all-start.2 = ((bf16[8,32,256]{2,1,0:T(8,128)(2,1)}), bf16[8,32,256]{2,1,0:T(8,128)(2,1)S(1)}, u32[]{:S(2)}, u32[]{:S(2)}) async-start(bf16[8,32,256]{2,1,0:T(8,128)(2,1)} %bitcast.20), calls=%async_computation.3 | async-start | bytes 262144 | tf_op jit(solution)/shard_map/all_to_all | solution.py:93
  86.8 21.8 %all-to-all-start.4 = ((bf16[32,32,256]{2,1,0:T(8,128)(2,1)}), bf16[32,32,256]{2,1,0:T(8,128)(2,1)S(1)}, u32[]{:S(2)}, u32[]{:S(2)}) async-start(bf16[32,32,256]{2,1,0:T(8,128)(2,1)} %broadcast_in_dim.106), calls=%async_computation.5 | async-start | bytes 1048576 | tf_op jit(solution)/shard_map/all_to_all | solution.py:12
  110.7 75.1 %all-to-all-start = ((bf16[32,48,1024]{2,1,0:T(8,128)(2,1)}), bf16[32,48,1024]{2,1,0:T(8,128)(2,1)}, u32[]{:S(2)}, u32[]{:S(2)}) async-start(bf16[32,48,1024]{2,1,0:T(8,128)(2,1)} %stack.21), calls=%async_computation | async-start | bytes 6291456 | tf_op jit(solution)/shard_map/all_to_all | solution.py:105
  186.7 25.5 %all-to-all-start.5 = ((bf16[32,32,256]{2,1,0:T(8,128)(2,1)}), bf16[32,32,256]{2,1,0:T(8,128)(2,1)S(1)}, u32[]{:S(2)}, u32[]{:S(2)}) async-start(bf16[32,32,256]{2,1,0:T(8,128)(2,1)} %broadcast_in_dim.107), calls=%async_computation.6 | async-start | bytes 1048576 | tf_op jit(solution)/shard_map/all_to_all | solution.py:12
  194.7 49.0 %reduce-scatter.2.cloned.1.call-start = ((), (), s32[]{:S(2)}) async-start(), calls=%async_computation.9 | async-start | bytes 1769472 | tf_op jit(solution)/shard_map/reduce_scatter | solution.py:119
  212.2 24.8 %copy-start.1 = (bf16[8192,256]{1,0:T(8,128)(2,1)S(1)}, bf16[8192,256]{1,0:T(8,128)(2,1)}, u32[]{:S(2)}) copy-start(bf16[8192,256]{1,0:T(8,128)(2,1)} %all-gather.2.cloned.1.call-done) | copy-start | bytes 12582916
  238.7 21.6 %all-to-all-start.7 = ((bf16[32,32,256]{2,1,0:T(8,128)(2,1)}), bf16[32,32,256]{2,1,0:T(8,128)(2,1)S(1)}, u32[]{:S(2)}, u32[]{:S(2)}) async-start(bf16[32,32,256]{2,1,0:T(8,128)(2,1)} %broadcast_in_dim.109), calls=%async_computation.8 | async-start | bytes 1048576 | tf_op jit(solution)/shard_map/all_to_all | solution.py:12
  263.3 0.6 copy-start.3
Sparse Core Ops, SparseCore 0:
  9.9 37.2 all-gather.1
  199.1 34.5 reduce-scatter.1
